TPU v7x, 512 devices: a whole 4x4x16 slice. The times are simulated.
512 devices in a mesh: seq: 64 (over z, y), chan: 8 (over x, core).
Axes of the slice: x: 4, y: 4, z: 16, core: 2. Of those that a mesh axis runs over, the one named last changes fastest.
Arguments:
- values: bfloat16 [16384, 4096], P('seq', 'chan'), may hold values from -6 to 6
- gates: bfloat16 [16384, 4096], P('seq', 'chan'), may hold values from -144 to 144
- filter_taps: bfloat16 [16384, 4096], P('seq', 'chan'), may hold values from -0.0625 to 0.0625, as said below
- skip_gain: float32 [4096], P('chan'), may hold values from -0.125 to 0.125
- out_weight: bfloat16 [4096, 2048], P('chan'), may hold values from -0.09375 to 0.09375
Outputs:
- projected: bfloat16 [2048, 16384], P('chan', 'seq')
Inputs may be any that keep to these rules, and one draw needn't show every extreme that they name: `filter_taps`: a causal filter for each channel.
All inputs are finite; a program needn't handle non-finite values.
Results may differ from a plain program's by a relative error of at most 0.0049.
Values may be sent and summed in bfloat16 or wider, within the bound.
A program may use at most 64 MiB of HBM per device.

v0:
```python
import math

import jax
import jax.numpy as jnp
from jax import lax
from jax.sharding import PartitionSpec as P

TWO_PI = 2.0 * math.pi
HIGH = lax.Precision.HIGHEST


def cut_along(array, dim, count):
    before, after = (array.shape[:dim], array.shape[dim + 1 :])
    return jnp.moveaxis(array.reshape(*before, count, -1, *after), dim, 0)


def sent_and_summed(array, axis, dim):
    pieces = cut_along(array, dim, lax.axis_size(axis))
    arrived = lax.all_to_all(pieces, axis, split_axis=0, concat_axis=0, tiled=True)
    return arrived.sum(axis=0)


def angle_table(first, second, period):
    product = first[:, None] * second[None, :] % period
    angles = product.astype(jnp.float32) * (TWO_PI / period)
    return (jnp.cos(angles), jnp.sin(angles))


def mix(equation, left, right):
    return jnp.einsum(equation, left, right, precision=HIGH)


def outer_forward(data, outer_cos, outer_sin, twist_cos, twist_sin, equation):
    source = data.astype(jnp.float32)
    real = mix(equation, outer_cos, source)
    imag = -mix(equation, outer_sin, source)
    cos_part = twist_cos[:, :, None]
    sin_part = twist_sin[:, :, None]
    return (real * cos_part + imag * sin_part, imag * cos_part - real * sin_part)


def inner_filter(spectra, inner_cos, inner_sin):
    value_re, value_im, taps_re, taps_im = spectra

    def forward(real, imag):
        out_re = mix("kr,jrc->jkc", inner_cos, real) + mix("kr,jrc->jkc", inner_sin, imag)
        out_im = mix("kr,jrc->jkc", inner_cos, imag) - mix("kr,jrc->jkc", inner_sin, real)
        return (out_re, out_im)

    value_fre, value_fim = forward(value_re, value_im)
    taps_fre, taps_fim = forward(taps_re, taps_im)
    prod_re = value_fre * taps_fre - value_fim * taps_fim
    prod_im = value_fre * taps_fim + value_fim * taps_fre
    back_re = mix("rk,jkc->jrc", inner_cos, prod_re) - mix("rk,jkc->jrc", inner_sin, prod_im)
    back_im = mix("rk,jkc->jrc", inner_cos, prod_im) + mix("rk,jkc->jrc", inner_sin, prod_re)
    return (back_re, back_im)


def untwist(real, imag, twist_cos, twist_sin):
    cos_part = twist_cos[:, :, None]
    sin_part = twist_sin[:, :, None]
    return (real * cos_part - imag * sin_part, imag * cos_part + real * sin_part)


def channels_plan(values, filter_taps):
    rows, width = values.shape
    blocks = lax.axis_size("seq")
    length = 2 * blocks * rows
    narrow = width // blocks
    whole_values, whole_taps = (
        lax.all_to_all(values, "seq", split_axis=1, concat_axis=0, tiled=True),
        lax.all_to_all(filter_taps, "seq", split_axis=1, concat_axis=0, tiled=True),
    )
    freq_ids = jnp.arange(2 * blocks, dtype=jnp.int32)
    block_ids = jnp.arange(blocks, dtype=jnp.int32)
    all_rows = jnp.arange(rows, dtype=jnp.int32)
    outer_cos, outer_sin = angle_table(freq_ids, block_ids, 2 * blocks)
    twist_cos, twist_sin = angle_table(freq_ids, all_rows, length)
    value_re, value_im = outer_forward(
        whole_values.reshape(blocks, rows, narrow),
        outer_cos,
        outer_sin,
        twist_cos,
        twist_sin,
        "ka,arc->krc",
    )
    taps_re, taps_im = outer_forward(
        whole_taps.reshape(blocks, rows, narrow),
        outer_cos,
        outer_sin,
        twist_cos,
        twist_sin,
        "ka,arc->krc",
    )
    inner_cos, inner_sin = angle_table(all_rows, all_rows, rows)
    back_re, back_im = inner_filter((value_re, value_im, taps_re, taps_im), inner_cos, inner_sin)
    turned_re, turned_im = untwist(back_re, back_im, twist_cos, twist_sin)
    final_cos, final_sin = angle_table(block_ids, freq_ids, 2 * blocks)
    signal = (
        mix("ak,krc->arc", final_cos, turned_re) - mix("ak,krc->arc", final_sin, turned_im)
    ) / length
    returned = lax.all_to_all(signal, "seq", split_axis=0, concat_axis=2, tiled=True)
    return returned[0]


def local(values, gates, filter_taps, skip_gain, out_weight):
    conv = channels_plan(values, filter_taps)
    gated = (
        gates.astype(jnp.float32) * (conv + skip_gain[None, :] * values.astype(jnp.float32))
    ).astype(jnp.bfloat16)
    projected = sent_and_summed(
        lax.dot_general(
            out_weight, gated, (((0,), (1,)), ((), ())), preferred_element_type=jnp.float32
        ),
        "chan",
        0,
    )
    return projected.astype(jnp.bfloat16)


def solution(mesh):
    placed = (P("seq", "chan"), P("seq", "chan"), P("seq", "chan"), P("chan"), P("chan", None))
    return jax.shard_map(
        local, mesh=mesh, in_specs=placed, out_specs=P("chan", "seq"), check_vma=False
    )
```

profile of v0, /device:TPU:1, one launch (start us, length us, event | category | flops | bytes accessed | tf_op | source)
XLA Modules:
  0.0 171.0 jit_solution(5254969974151336605)
XLA Ops:
  0.0 1.9 %copy.16 = bf16[256,512]{0,1:T(8,128)(2,1)} copy(bf16[256,512]{1,0:T(8,128)(2,1)} %param.7) | data formatting | bytes 524288 | tf_op args[2]
  1.9 19.3 %all-to-all-start.1 = ((bf16[256,64,8]{0,2,1:T(8,128)(2,1)}), bf16[256,64,8]{0,2,1:T(8,128)(2,1)S(1)}, u32[]{:S(2)}, u32[]{:S(2)}) async-start(bf16[256,64,8]{0,2,1:T(8,128)(2,1)} %bitcast.7), calls=%async_computation.1 | async-start | bytes 524288 | tf_op jit(solution)/shard_map/all_to_all | solution.py:72
  21.2 1.8 %copy.14 = bf16[256,512]{0,1:T(8,128)(2,1)} copy(bf16[256,512]{1,0:T(8,128)(2,1)} %param.5) | data formatting | bytes 524288 | tf_op args[0]
  23.5 17.2 %all-to-all-done.1 = bf16[256,64,8]{0,2,1:T(8,128)(2,1)S(1)} async-done(((bf16[256,64,8]{0,2,1:T(8,128)(2,1)}), bf16[256,64,8]{0,2,1:T(8,128)(2,1)S(1)}, u32[]{:S(2)}, u32[]{:S(2)}) %all-to-all-start.1) | async-done | bytes 262176 | tf_op jit(solution)/shard_map/all_to_all | solution.py:72
  40.7 0.7 copy-done.5
  41.4 7.5 %all-to-all-start = ((bf16[256,64,8]{0,2,1:T(8,128)(2,1)}), bf16[256,64,8]{0,2,1:T(8,128)(2,1)}, u32[]{:S(2)}, u32[]{:S(2)}) async-start(bf16[256,64,8]{0,2,1:T(8,128)(2,1)} %bitcast.2), calls=%async_computation | async-start | bytes 524288 | tf_op jit(solution)/shard_map/all_to_all | solution.py:71
  48.9 1.7 convolution_negate_fusion
  50.6 1.7 fusion.28
  52.3 3.0 %fusion.42 = f32[128,8,256]{2,0,1:T(8,128)} fusion(f32[128,256,8]{1,0,2:T(8,128)S(1)} %convolution_negate_fusion, f32[128,256,8]{1,0,2:T(8,128)S(1)} %fusion.28, f32[128,256]{1,0:T(8,128)S(1)} %get-tuple-element.7, f32[128,256]{1,0:T(8,128)S(1)} %get-tuple-element.8), kind=kOutput, calls=%fused_computation.61 | convolution fusion | flops 807010304 | bytes 3407872 | tf_op jit(solution)/shard_map/kr,jrc->jkc/dot_general | solution.py:30
  55.3 3.0 %fusion.38 = f32[128,8,256]{2,0,1:T(8,128)} fusion(f32[128,256,8]{1,0,2:T(8,128)S(1)} %fusion.28, f32[128,256,8]{1,0,2:T(8,128)S(1)} %convolution_negate_fusion, f32[128,256]{1,0:T(8,128)S(1)} %get-tuple-element.7, f32[128,256]{1,0:T(8,128)S(1)} %get-tuple-element.8), kind=kOutput, calls=%fused_computation.57 | convolution fusion | flops 807010304 | bytes 3407872 | tf_op jit(solution)/shard_map/kr,jrc->jkc/dot_general | solution.py:30
  58.2 8.8 %all-to-all-done = bf16[256,64,8]{0,2,1:T(8,128)(2,1)} async-done(((bf16[256,64,8]{0,2,1:T(8,128)(2,1)}), bf16[256,64,8]{0,2,1:T(8,128)(2,1)}, u32[]{:S(2)}, u32[]{:S(2)}) %all-to-all-start) | async-done | bytes 262176 | tf_op jit(solution)/shard_map/all_to_all | solution.py:71
  67.0 1.7 convolution_negate_fusion.1
  68.7 1.7 fusion.47
  70.4 2.0 %fusion.44 = f32[128,8,256]{2,0,1:T(8,128)S(1)} fusion(f32[128,256,8]{1,0,2:T(8,128)S(1)} %convolution_negate_fusion.1, f32[128,256,8]{1,0,2:T(8,128)S(1)} %fusion.47, f32[128,256]{1,0:T(8,128)S(1)} %get-tuple-element.7, f32[128,256]{1,0:T(8,128)S(1)} %get-tuple-element.8), kind=kOutput, calls=%fused_computation.63 | convolution fusion | flops 807010304 | bytes 3407872 | tf_op jit(solution)/shard_map/kr,jrc->jkc/dot_general | solution.py:30
  72.5 2.0 %fusion.40 = f32[128,8,256]{2,0,1:T(8,128)S(1)} fusion(f32[128,256,8]{1,0,2:T(8,128)S(1)} %fusion.47, f32[128,256,8]{1,0,2:T(8,128)S(1)} %convolution_negate_fusion.1, f32[128,256]{1,0:T(8,128)S(1)} %get-tuple-element.7, f32[128,256]{1,0:T(8,128)S(1)} %get-tuple-element.8), kind=kOutput, calls=%fused_computation.59 | convolution fusion | flops 807010304 | bytes 3407872 | tf_op jit(solution)/shard_map/kr,jrc->jkc/dot_general | solution.py:30
  74.5 2.3 %convolution_add_fusion.1 = f32[128,8,256]{2,0,1:T(8,128)S(1)} fusion(f32[128,8,256]{2,0,1:T(8,128)S(1)} %copy-done.4, f32[128,256,8]{1,0,2:T(8,128)S(1)} %copy-done.2, f32[128,256,8]{1,0,2:T(8,128)S(1)} %convolution_negate_fusion, f32[128,256]{1,0:T(8,128)S(1)} %get-tuple-element.7, f32[128,256]{1,0:T(8,128)S(1)} %get-tuple-element.8), kind=kOutput, calls=%fused_computation.7 | convolution fusion | flops 807272448 | bytes 4456448 | tf_op jit(solution)/shard_map/kr,jrc->jkc/dot_general | solution.py:30
  76.8 2.1 %convolution_add_fusion.2 = f32[128,8,256]{2,0,1:T(8,128)S(1)} fusion(f32[128,8,256]{2,0,1:T(8,128)S(1)} %fusion.44, f32[128,256,8]{1,0,2:T(8,128)S(1)} %fusion.47, f32[128,256,8]{1,0,2:T(8,128)S(1)} %convolution_negate_fusion.1, f32[128,256]{1,0:T(8,128)S(1)} %get-tuple-element.7, f32[128,256]{1,0:T(8,128)S(1)} %get-tuple-element.8), kind=kOutput, calls=%fused_computation.8 | convolution fusion | flops 807272448 | bytes 4456448 | tf_op jit(solution)/shard_map/kr,jrc->jkc/dot_general | solution.py:30
  78.9 2.0 %convolution_subtract_fusion.1 = f32[128,8,256]{2,0,1:T(8,128)S(1)} fusion(f32[128,8,256]{2,0,1:T(8,128)S(1)} %copy-done.3, f32[128,256,8]{1,0,2:T(8,128)S(1)} %convolution_negate_fusion, f32[128,256,8]{1,0,2:T(8,128)S(1)} %copy-done.2, f32[128,256]{1,0:T(8,128)S(1)} %get-tuple-element.7, f32[128,256]{1,0:T(8,128)S(1)} %get-tuple-element.8), kind=kOutput, calls=%fused_computation.5 | convolution fusion | flops 807272448 | bytes 4456448 | tf_op jit(solution)/shard_map/kr,jrc->jkc/dot_general | solution.py:30
  81.0 2.3 %multiply_subtract_fusion = (f32[128,8,256]{2,0,1:T(8,128)S(1)}, f32[128,8,256]{2,0,1:T(8,128)S(1)}) fusion(f32[128,8,256]{2,0,1:T(8,128)S(1)} %convolution_subtract_fusion.1, f32[128,8,256]{2,0,1:T(8,128)S(1)} %convolution_add_fusion.2, f32[128,8,256]{2,0,1:T(8,128)S(1)} %convolution_add_fusion.1, f32[128,8,256]{2,0,1:T(8,128)S(1)} %fusion.40, ...), kind=kOutput, calls=%fused_computation.27 | convolution fusion | flops 808845312 | bytes 8650752 | tf_op jit(solution)/shard_map/kr,jrc->jkc/dot_general | solution.py:30
  83.2 2.0 %fusion.8 = f32[128,8,256]{2,0,1:T(8,128)S(1)} fusion(f32[128,8,256]{2,0,1:T(8,128)S(1)} %get-tuple-element.5), kind=kOutput, calls=%fused_computation.18 | convolution fusion | flops 806223872 | bytes 2097152 | tf_op jit(solution)/shard_map/rk,jkc->jrc/dot_general | solution.py:30
  85.2 2.0 %fusion.4 = f32[128,8,256]{2,0,1:T(8,128)S(1)} fusion(f32[128,8,256]{2,0,1:T(8,128)S(1)} %get-tuple-element.6), kind=kOutput, calls=%fused_computation.14 | convolution fusion | flops 806223872 | bytes 2097152 | tf_op jit(solution)/shard_map/rk,jkc->jrc/dot_general | solution.py:30
  87.2 2.2 %convolution_subtract_fusion = f32[128,8,256]{2,0,1:T(8,128)S(1)} fusion(f32[128,8,256]{2,0,1:T(8,128)S(1)} %fusion.8, f32[128,8,256]{2,0,1:T(8,128)S(1)} %get-tuple-element.6), kind=kOutput, calls=%fused_computation.4 | convolution fusion | flops 806486016 | bytes 3145728 | tf_op jit(solution)/shard_map/rk,jkc->jrc/dot_general | solution.py:30
  89.4 2.0 %convolution_add_fusion = f32[128,8,256]{2,0,1:T(8,128)S(1)} fusion(f32[128,8,256]{2,0,1:T(8,128)S(1)} %fusion.4, f32[128,8,256]{2,0,1:T(8,128)S(1)} %get-tuple-element.5), kind=kOutput, calls=%fused_computation.3 | convolution fusion | flops 806486016 | bytes 3145728 | tf_op jit(solution)/shard_map/rk,jkc->jrc/dot_general | solution.py:30
  91.4 0.9 fusion.2
  92.3 0.9 fusion
  93.3 1.1 copy.18
  94.4 7.9 %all-to-all-start.2 = ((f32[64,256,8]{1,2,0:T(8,128)}), f32[64,256,8]{1,2,0:T(8,128)S(1)}, u32[]{:S(2)}, u32[]{:S(2)}) async-start(f32[64,256,8]{1,2,0:T(8,128)} %copy.18), calls=%async_computation.2 | async-start | bytes 1048576 | tf_op jit(solution)/shard_map/all_to_all | solution.py:102
  102.5 28.8 %all-to-all-done.2 = f32[64,256,8]{1,2,0:T(8,128)S(1)} async-done(((f32[64,256,8]{1,2,0:T(8,128)}), f32[64,256,8]{1,2,0:T(8,128)S(1)}, u32[]{:S(2)}, u32[]{:S(2)}) %all-to-all-start.2) | async-done | bytes 524320 | tf_op jit(solution)/shard_map/all_to_all | solution.py:102
  131.3 1.8 %fusion.25 = f32[256,2048]{1,0:T(8,128)S(1)} fusion(bf16[512,2048]{1,0:T(8,128)(2,1)S(1)} %copy-done, f32[64,256,8]{1,2,0:T(8,128)S(1)} %all-to-all-done.2, bf16[256,512]{0,1:T(8,128)(2,1)} %copy.14, bf16[256,512]{0,1:T(8,128)(2,1)S(1)} %copy.13, f32[512]{0:T(512)S(1)} %copy-done.7), kind=kOutput, calls=%fused_computation.45 | convolution fusion | flops 537657344 | bytes 5244928 | tf_op jit(solution)/shard_map/dot_general | solution.py:112
  133.3 35.2 %all_to_all.52 = f32[8,256,256]{1,2,0:T(8,128)} all-to-all(f32[8,256,256]{1,2,0:T(8,128)S(1)} %bitcast.90), channel_id=1, replica_groups=mesh['seq'=64,'chan'=8] {'chan'}, dimensions={0} | all-to-all | bytes 4194304 | tf_op jit(solution)/shard_map/all_to_all | solution.py:19
  168.5 1.7 %reduce_sum.9 = bf16[256,256]{0,1:T(8,128)(2,1)S(1)} reduce(f32[8,256,256]{1,2,0:T(8,128)} %all_to_all.52, f32[]{:T(128)} %constant.62.clone.1), dimensions={0}, to_apply=%region_0.1 | reduce | flops 458752 | bytes 2228228 | tf_op jit(solution)/shard_map/reduce_sum | solution.py:20
  170.2 0.8 copy.22
  (18 shorter events, 0.9 us)
Async XLA Ops:
  0.0 131.3 %copy-start = (bf16[512,2048]{1,0:T(8,128)(2,1)S(1)}, bf16[512,2048]{1,0:T(8,128)(2,1)}, u32[]{:S(2)}) copy-start(bf16[512,2048]{1,0:T(8,128)(2,1)} %param.9) | copy-start | bytes 6291460
  1.9 38.8 %all-to-all-start.1 = ((bf16[256,64,8]{0,2,1:T(8,128)(2,1)}), bf16[256,64,8]{0,2,1:T(8,128)(2,1)S(1)}, u32[]{:S(2)}, u32[]{:S(2)}) async-start(bf16[256,64,8]{0,2,1:T(8,128)(2,1)} %bitcast.7), calls=%async_computation.1 | async-start | bytes 524288 | tf_op jit(solution)/shard_map/all_to_all | solution.py:72
  40.7 0.7 copy-start.5
  41.4 25.6 %all-to-all-start = ((bf16[256,64,8]{0,2,1:T(8,128)(2,1)}), bf16[256,64,8]{0,2,1:T(8,128)(2,1)}, u32[]{:S(2)}, u32[]{:S(2)}) async-start(bf16[256,64,8]{0,2,1:T(8,128)(2,1)} %bitcast.2), calls=%async_computation | async-start | bytes 524288 | tf_op jit(solution)/shard_map/all_to_all | solution.py:71
  52.3 3.0 %copy-start.1 = (f32[128,256,8]{1,0,2:T(8,128)}, f32[128,256,8]{1,0,2:T(8,128)S(1)}, u32[]{:S(2)}) copy-start(f32[128,256,8]{1,0,2:T(8,128)S(1)} %fusion.28) | copy-start | bytes 3145732
  72.5 2.1 %copy-start.2 = (f32[128,256,8]{1,0,2:T(8,128)S(1)}, f32[128,256,8]{1,0,2:T(8,128)}, u32[]{:S(2)}) copy-start(f32[128,256,8]{1,0,2:T(8,128)} %copy-done.1) | copy-start | bytes 3145732
  72.5 2.1 %copy-start.4 = (f32[128,8,256]{2,0,1:T(8,128)S(1)}, f32[128,8,256]{2,0,1:T(8,128)}, u32[]{:S(2)}) copy-start(f32[128,8,256]{2,0,1:T(8,128)} %fusion.42) | copy-start | bytes 3145732
  76.8 2.1 %copy-start.3 = (f32[128,8,256]{2,0,1:T(8,128)S(1)}, f32[128,8,256]{2,0,1:T(8,128)}, u32[]{:S(2)}) copy-start(f32[128,8,256]{2,0,1:T(8,128)} %fusion.38) | copy-start | bytes 3145732
  92.3 10.0 %copy-start.6 = (bf16[256,512]{1,0:T(8,128)(2,1)S(1)}, bf16[256,512]{1,0:T(8,128)(2,1)}, u32[]{:S(2)}) copy-start(bf16[256,512]{1,0:T(8,128)(2,1)} %param.6) | copy-start | bytes 786436
  93.3 38.0 %copy-start.7 = (f32[512]{0:T(512)S(1)}, f32[512]{0:T(512)}, u32[]{:S(2)}) copy-start(f32[512]{0:T(512)} %param.8) | copy-start | bytes 6148
  94.4 36.9 %all-to-all-start.2 = ((f32[64,256,8]{1,2,0:T(8,128)}), f32[64,256,8]{1,2,0:T(8,128)S(1)}, u32[]{:S(2)}, u32[]{:S(2)}) async-start(f32[64,256,8]{1,2,0:T(8,128)} %copy.18), calls=%async_computation.2 | async-start | bytes 1048576 | tf_op jit(solution)/shard_map/all_to_all | solution.py:102
where the time goes:
time: 172 us; the launch traced here: 171 us
  waiting for transfers between devices  54.7 us (32%)
  matrix products  37.2 us (22%)
  blocking collectives  35.2 us (20%)
  starting transfers between devices  34.7 us (20%)
  local copies, waits for them, and re-layouts  6.64 us (4%)
  other arithmetic  2.26 us (1%)
    dot_general x18, matrix products, mix(): return jnp.einsum(equation, left, right, precision=HIGH)  35.4 us
    all_to_all x1, blocking collectives, sent_and_summed(): lax.all_to_all(pieces, axis, split_axis=0, concat_axis=0, tiled=True)  35.2 us
    all_to_all x1, waiting for transfers between devices, channels_plan(): lax.all_to_all(signal, 'seq', split_axis=0, concat_axis=2, tiled=True)  28.8 us
    all_to_all x1, starting transfers between devices, channels_plan(): lax.all_to_all(filter_taps, 'seq', split_axis=1, concat_axis=0, tiled=True)  19.3 us
    all_to_all x1, waiting for transfers between devices, channels_plan(): lax.all_to_all(filter_taps, 'seq', split_axis=1, concat_axis=0, tiled=True)  17.2 us
    all_to_all x1, waiting for transfers between devices, channels_plan(): lax.all_to_all(values, 'seq', split_axis=1, concat_axis=0, tiled=True)  8.77 us
    all_to_all x1, starting transfers between devices, channels_plan(): lax.all_to_all(signal, 'seq', split_axis=0, concat_axis=2, tiled=True)  7.93 us
    all_to_all x1, starting transfers between devices, channels_plan(): lax.all_to_all(values, 'seq', split_axis=1, concat_axis=0, tiled=True)  7.49 us
  transfers between devices with their start and end apart: 3, of which 3 were waited for; matrix products, arithmetic and copies ran while one was open for 7% of the time, Pallas kernels for 0%

commit v1 on v0

v1 whole, which is shorter than its diff:
```python
import functools

import jax
import jax.numpy as jnp
import numpy as np
from jax import lax
from jax.experimental import pallas as pl
from jax.experimental.pallas import tpu as pltpu
from jax.sharding import PartitionSpec as P

MESH = pl.DeviceIdType.MESH
F32 = jnp.float32
BF16 = jnp.bfloat16


def split_table(table):
    high = table.astype(np.float32).astype(BF16)
    low = (table - high.astype(np.float64)).astype(np.float32).astype(BF16)
    return high, low


def tables(blocks, rows):
    ids = np.arange(blocks)
    turn = ids[:, None] * (2 * ids[None, :] + 1) % (4 * blocks) * (2 * np.pi / (4 * blocks))
    outer = np.concatenate([np.cos(turn).T, -np.sin(turn).T], axis=0)
    final = np.concatenate([np.cos(turn), -np.sin(turn)], axis=1) / (blocks * rows)
    r = np.arange(rows)
    twist = (2 * ids[:, None] + 1) * r[None, :] * (np.pi / (2 * blocks * rows))
    inner = r[:, None] * r[None, :] % rows * (2 * np.pi / rows)
    c, s = np.cos(inner), np.sin(inner)
    full = np.concatenate(
        [np.concatenate([c, -s], axis=1), np.concatenate([s, c], axis=1)], axis=0
    )
    return (
        np.stack(split_table(outer)),
        np.stack(split_table(full)),
        np.stack(split_table(final)),
        np.stack([np.cos(twist), np.sin(twist)]).astype(np.float32),
    )


def mm(left, right):
    return jnp.dot(left, right, preferred_element_type=F32)


def halves(x):
    high = x.astype(BF16)
    return high, (x - high.astype(F32)).astype(BF16)


def mm3(left, right_ref):
    high, low = halves(left)
    return mm(high, right_ref[0]) + mm(low, right_ref[0]) + mm(high, right_ref[1])


def kernel(
    blocks, lanes,
    values_hbm, gates_hbm, taps_hbm, skip_hbm, weight_hbm,
    outer_hbm, full_hbm, final_hbm, twist_hbm,
    out_hbm,
    values_ref, gates_ref, taps_ref, skip_ref, weight_ref,
    outer_ref, full_ref, final_ref, twist_ref,
    sbuf, rbuf, xf, yf, obuf, cbuf, gt, wt, pbuf, qbuf, fin,
    load_sem, send1, recv1, send2, recv2, send3, recv3, own_sem,
):
    me = lax.axis_index("seq")
    mine = lax.axis_index("chan")
    rows, width = values_ref.shape
    narrow = width // blocks

    loads = []
    for index, (source, target) in enumerate(
        (
            (values_hbm, values_ref),
            (taps_hbm, taps_ref),
            (gates_hbm, gates_ref),
            (skip_hbm, skip_ref),
            (weight_hbm, weight_ref),
            (outer_hbm, outer_ref),
            (full_hbm, full_ref),
            (final_hbm, final_ref),
            (twist_hbm, twist_ref),
        )
    ):
        copy = pltpu.make_async_copy(source, target, load_sem.at[index])
        copy.start()
        loads.append(copy)

    barrier = pltpu.get_barrier_semaphore()

    def greet_seq(step, carry):
        pl.semaphore_signal(
            barrier, inc=1, device_id=(lax.rem(me + step, blocks), mine), device_id_type=MESH
        )
        return carry

    def greet_chan(step, carry):
        pl.semaphore_signal(
            barrier, inc=1, device_id=(me, lax.rem(mine + step, lanes)), device_id_type=MESH
        )
        return carry

    lax.fori_loop(1, blocks, greet_seq, 0)
    lax.fori_loop(1, lanes, greet_chan, 0)

    part = 256
    row_ids = lax.broadcasted_iota(jnp.int32, (part, part), 0)
    col_ids = lax.broadcasted_iota(jnp.int32, (part, part), 1)
    eye = jnp.where(row_ids == col_ids, 1.0, 0.0).astype(BF16)

    def turned(block):
        return lax.dot_general(eye, block, (((1,), (1,)), ((), ())), preferred_element_type=F32)

    loads[0].wait()
    loads[1].wait()
    per = part // narrow
    for b in range(width // part):
        columns = slice(b * part, (b + 1) * part)
        v = turned(values_ref[:, columns])
        h = turned(taps_ref[:, columns])
        both = jnp.concatenate(
            [v.reshape(per, narrow, rows), h.reshape(per, narrow, rows)], axis=1
        )
        sbuf[b * per : (b + 1) * per] = both.astype(BF16)

    pl.semaphore_wait(barrier, blocks + lanes - 2)

    def send_first(step, carry):
        peer = lax.rem(me + step, blocks)
        pltpu.make_async_remote_copy(
            src_ref=sbuf.at[peer], dst_ref=rbuf.at[me], send_sem=send1, recv_sem=recv1,
            device_id=(peer, mine), device_id_type=MESH,
        ).start()
        return carry

    lax.fori_loop(1, blocks, send_first, 0)
    own = pltpu.make_async_copy(sbuf.at[me], rbuf.at[me], own_sem.at[0])
    own.start()

    loads[2].wait()
    for b in range(width // part):
        columns = slice(b * part, (b + 1) * part)
        gt[columns, :] = turned(gates_ref[:, columns])
    loads[4].wait()
    for j in range(lanes):
        wt[j] = turned(weight_ref[:, j * part : (j + 1) * part]).astype(BF16)
    for index in (3, 5, 6, 7, 8):
        loads[index].wait()

    own.wait()
    rest = pl.ds(0, blocks - 1)
    pltpu.make_async_copy(rbuf.at[rest], rbuf.at[rest], recv1).wait()

    arrived = rbuf[...].astype(F32).reshape(blocks * 2 * narrow, rows)
    lane = rows // 2
    xf[0] = arrived[:, :lane]
    xf[1] = arrived[:, lane:]
    cos_t, sin_t = twist_ref[0], twist_ref[1]
    cos_2 = jnp.concatenate([cos_t, cos_t], axis=1)
    sin_2 = jnp.concatenate([sin_t, sin_t], axis=1)
    group = narrow // 2
    lines = group * blocks

    def half(g, carry):
        streams = ([], [])
        for c in range(group):
            channel = g * group + c
            x = jnp.concatenate(
                [
                    xf[side, pl.ds(start + channel, blocks, stride=2 * narrow), :]
                    for start in (0, narrow)
                    for side in range(2)
                ],
                axis=1,
            ).astype(BF16)
            y = mm(outer_ref[0], x) + mm(outer_ref[1], x)
            re, im = y[:blocks], y[blocks:]
            real = re * cos_2 + im * sin_2
            imag = im * cos_2 - re * sin_2
            for stream in range(2):
                cut = slice(stream * rows, (stream + 1) * rows)
                streams[stream].append(jnp.concatenate([real[:, cut], imag[:, cut]], axis=1))
        spectra = mm3(jnp.concatenate(streams[0] + streams[1], axis=0), full_ref)
        vre, vim = spectra[:lines, :rows], spectra[:lines, rows:]
        direct = [
            jnp.broadcast_to(skip_ref[pl.ds(me * narrow + g * group + c, 1), :], (blocks, rows))
            for c in range(group)
        ]
        hre = spectra[lines:, :rows] + jnp.concatenate(direct, axis=0)
        him = spectra[lines:, rows:]
        product = jnp.concatenate([vre * hre - vim * him, -(vre * him + vim * hre)], axis=1)
        back = mm3(product, full_ref)
        wide = []
        for c in range(group):
            cut = slice(c * blocks, (c + 1) * blocks)
            re, im = back[cut, :rows], -back[cut, rows:]
            wide.append(
                jnp.concatenate([re * cos_t - im * sin_t, im * cos_t + re * sin_t], axis=0)
            )
        high, low = halves(jnp.concatenate(wide, axis=1))
        signal = mm(final_ref[0], high) + mm(final_ref[0], low) + mm(final_ref[1], high)
        for c in range(group):
            for side in range(2):
                start = c * rows + side * lane
                yf[side, pl.ds(g * group + c, blocks, stride=narrow), :] = signal[
                    :, start : start + lane
                ]
        return carry

    lax.fori_loop(0, 2, half, 0)
    result = jnp.concatenate([yf[0], yf[1]], axis=1)
    obuf[...] = result.reshape(blocks, narrow, rows).astype(BF16)

    def send_second(step, carry):
        peer = lax.rem(me + step, blocks)
        pltpu.make_async_remote_copy(
            src_ref=obuf.at[peer], dst_ref=cbuf.at[me], send_sem=send2, recv_sem=recv2,
            device_id=(peer, mine), device_id_type=MESH,
        ).start()
        return carry

    lax.fori_loop(1, blocks, send_second, 0)
    own = pltpu.make_async_copy(obuf.at[me], cbuf.at[me], own_sem.at[1])
    own.start()
    own.wait()
    pltpu.make_async_copy(cbuf.at[rest], cbuf.at[rest], recv2).wait()

    conv = cbuf[...].astype(F32).reshape(width, rows)
    gated = (gt[...] * conv).astype(BF16)

    def send_third(step, carry):
        peer = lax.rem(mine + step, lanes)
        pbuf[peer] = mm(wt[peer], gated).astype(BF16)
        pltpu.make_async_remote_copy(
            src_ref=pbuf.at[peer], dst_ref=qbuf.at[mine], send_sem=send3, recv_sem=recv3,
            device_id=(me, peer), device_id_type=MESH,
        ).start()
        return carry

    lax.fori_loop(1, lanes, send_third, 0)
    total = mm(wt[mine], gated)
    others = pl.ds(0, lanes - 1)
    pltpu.make_async_copy(qbuf.at[others], qbuf.at[others], recv3).wait()

    def add(step, running):
        return running + qbuf[lax.rem(mine + step, lanes)].astype(F32)

    for step in range(1, lanes):
        total = add(step, total)
    fin[...] = total.astype(BF16)
    done = pltpu.make_async_copy(fin, out_hbm, own_sem.at[2])
    done.start()
    pltpu.make_async_copy(sbuf.at[rest], sbuf.at[rest], send1).wait()
    pltpu.make_async_copy(obuf.at[rest], obuf.at[rest], send2).wait()
    pltpu.make_async_copy(pbuf.at[others], pbuf.at[others], send3).wait()
    done.wait()


def local(blocks, lanes, values, gates, taps, skip, weight):
    rows, width = values.shape
    depth, features = weight.shape
    narrow = width // blocks
    outer, full, final, twist = tables(blocks, rows)
    anywhere = pl.BlockSpec(memory_space=pl.ANY)
    vmem = pltpu.VMEM
    dma = pltpu.SemaphoreType.DMA
    operands = (values, gates, taps, skip[:, None], weight, outer, full, final, twist)
    return pl.pallas_call(
        functools.partial(kernel, blocks, lanes),
        out_shape=jax.ShapeDtypeStruct((features // lanes, rows), BF16),
        in_specs=[anywhere] * len(operands),
        out_specs=anywhere,
        scratch_shapes=[
            vmem(values.shape, BF16),
            vmem(gates.shape, BF16),
            vmem(taps.shape, BF16),
            vmem((width, 1), F32),
            vmem(weight.shape, BF16),
            vmem(outer.shape, BF16),
            vmem(full.shape, BF16),
            vmem(final.shape, BF16),
            vmem(twist.shape, F32),
            vmem((blocks, 2 * narrow, rows), BF16),
            vmem((blocks, 2 * narrow, rows), BF16),
            vmem((2, blocks * 2 * narrow, rows // 2), F32),
            vmem((2, blocks * narrow, rows // 2), F32),
            vmem((blocks, narrow, rows), BF16),
            vmem((blocks, narrow, rows), BF16),
            vmem((width, rows), F32),
            vmem((lanes, features // lanes, depth), BF16),
            vmem((lanes, features // lanes, rows), BF16),
            vmem((lanes, features // lanes, rows), BF16),
            vmem((features // lanes, rows), BF16),
            dma((9,)), dma, dma, dma, dma, dma, dma, dma((3,)),
        ],
        compiler_params=pltpu.CompilerParams(
            collective_id=0, has_side_effects=True, vmem_limit_bytes=56 * 2**20
        ),
        name="hyena",
    )(*operands)


def solution(mesh):
    placed = (P("seq", "chan"), P("seq", "chan"), P("seq", "chan"), P("chan"), P("chan", None))
    body = functools.partial(local, mesh.shape["seq"], mesh.shape["chan"])
    return jax.shard_map(
        body, mesh=mesh, in_specs=placed, out_specs=P("chan", "seq"), check_vma=False
    )
```

time: 172 us -> 80.7 us (0.47)
  Pallas kernels: 0 us -> 77.5 us
  waiting for transfers between devices: 54.7 us -> 0 us
  matrix products: 37.2 us -> 0 us
  blocking collectives: 35.2 us -> 0 us
  starting transfers between devices: 34.7 us -> 0 us
  local copies, waits for them, and re-layouts: 6.64 us -> 3.09 us
  other arithmetic: 2.26 us -> 0 us
    pallas_call x0 -> x1, Pallas kernels: none -> 77.5 us  [local(): pl.pallas_call(functools.partial(kernel, blocks, lanes), out_shape=jax.Sh...]
    all_to_all x3 -> x0, waiting for transfers between devices: 54.7 us -> none  [the longest x1 28.8 us: channels_plan(): lax.all_to_all(signal, 'seq', split_axis=0, concat_axis=2, tiled=True)]
    dot_general x19 -> x0, matrix products: 37.2 us -> none  [the longest x18 35.4 us: mix(): return jnp.einsum(equation, left, right, precision=HIGH)]
    all_to_all x1 -> x0, blocking collectives: 35.2 us -> none  [sent_and_summed(): lax.all_to_all(pieces, axis, split_axis=0, concat_axis=0, tiled=True)]
    all_to_all x3 -> x0, starting transfers between devices: 34.7 us -> none  [the longest x1 19.3 us: channels_plan(): lax.all_to_all(filter_taps, 'seq', split_axis=1, concat_axis=0, tiled=True)]
    unnamed x19 -> x1, local copies, waits for them, and re-layouts: 4.59 us -> 1.57 us
    reduce_sum x1 -> x0, other arithmetic: 1.74 us -> none  [sent_and_summed(): return arrived.sum(axis=0)]
  transfers between devices with their start and end apart: 3 -> 0, of which waited for: 3 -> 0; matrix products, arithmetic and copies ran while one was open for 7% -> 0% of each run, Pallas kernels for 0% -> 0%
where the time goes in v1:
time: 80.7 us; the launch traced here: 80.6 us
  Pallas kernels  77.5 us (96%)
  local copies, waits for them, and re-layouts  3.09 us (4%)
    pallas_call x1, Pallas kernels, local(): pl.pallas_call(functools.partial(kernel, blocks, lanes), out_shape=jax.Sh...  77.5 us

profile of v1, /device:TPU:1, one launch (start us, length us, event | category | flops | bytes accessed | tf_op | source)
XLA Modules:
  0.0 80.6 jit_solution(4441832647367161393)
XLA Ops:
  0.0 1.5 %copy.10.skip_hbm = f32[512,1]{1,0:T(8,128)} copy(f32[512,1]{0,1:T(1,128)} %bitcast.1) | data formatting | bytes 4096 | tf_op jit(solution)/shard_map/broadcast_in_dim | solution.py:267
  1.5 77.5 %hyena.1 = bf16[256,256]{1,0:T(8,128)(2,1)} custom-call(bf16[256,512]{1,0:T(8,128)(2,1)} %values_hbm.1, bf16[256,512]{1,0:T(8,128)(2,1)} %gates_hbm.1, bf16[256,512]{1,0:T(8,128)(2,1)} %taps_hbm.1, f32[512,1]{1,0:T(8,128)} %copy.10.skip_hbm, bf16[512,2048]{1,0:T(8,128)(2,1)} %weight_hbm.1, bf16[2,128,64]{2,1,0:T(8,128)(2,1)} %constant.8.clone.outer_hbm, ...), custom_call_target="tpu_custom_call" | custom-call | tf_op jit(solution)/shard_map/hyena/pallas_call | solution.py:268
  79.0 1.6 %copy.12 = bf16[256,256]{1,0:T(8,128)(2,1)} copy(bf16[256,256]{1,0:T(8,128)(2,1)} %hyena.1) | data formatting | bytes 262144

commit v2 on v1

--- a/solution.py
+++ b/solution.py
@@ -55,10 +55,10 @@
 
 def kernel(
     blocks, lanes,
-    values_hbm, gates_hbm, taps_hbm, skip_hbm, weight_hbm,
+    values_hbm, gates_hbm, taps_hbm, skip_ref, weight_hbm,
     outer_hbm, full_hbm, final_hbm, twist_hbm,
     out_hbm,
-    values_ref, gates_ref, taps_ref, skip_ref, weight_ref,
+    values_ref, gates_ref, taps_ref, weight_ref,
     outer_ref, full_ref, final_ref, twist_ref,
     sbuf, rbuf, xf, yf, obuf, cbuf, gt, wt, pbuf, qbuf, fin,
     load_sem, send1, recv1, send2, recv2, send3, recv3, own_sem,
@@ -74,7 +74,6 @@
             (values_hbm, values_ref),
             (taps_hbm, taps_ref),
             (gates_hbm, gates_ref),
-            (skip_hbm, skip_ref),
             (weight_hbm, weight_ref),
             (outer_hbm, outer_ref),
             (full_hbm, full_ref),
@@ -114,61 +113,83 @@
     loads[0].wait()
     loads[1].wait()
     per = part // narrow
+    group = narrow // 2
+    row_of = lax.broadcasted_iota(jnp.int32, (per, narrow, rows), 1)
+
+    def paired(first, second):
+        low = row_of[: first.shape[0], :, : first.shape[2]] < group
+        return (
+            jnp.where(low, first, pltpu.roll(second, group, 1)),
+            jnp.where(low, pltpu.roll(first, group, 1), second),
+        )
+
     for b in range(width // part):
         columns = slice(b * part, (b + 1) * part)
         v = turned(values_ref[:, columns])
         h = turned(taps_ref[:, columns])
-        both = jnp.concatenate(
-            [v.reshape(per, narrow, rows), h.reshape(per, narrow, rows)], axis=1
-        )
-        sbuf[b * per : (b + 1) * per] = both.astype(BF16)
+        both = paired(v.reshape(per, narrow, rows), h.reshape(per, narrow, rows))
+        for g in range(2):
+            sbuf[g, b * per : (b + 1) * per] = both[g].astype(BF16)
 
     pl.semaphore_wait(barrier, blocks + lanes - 2)
 
-    def send_first(step, carry):
-        peer = lax.rem(me + step, blocks)
-        pltpu.make_async_remote_copy(
-            src_ref=sbuf.at[peer], dst_ref=rbuf.at[me], send_sem=send1, recv_sem=recv1,
-            device_id=(peer, mine), device_id_type=MESH,
-        ).start()
-        return carry
-
-    lax.fori_loop(1, blocks, send_first, 0)
-    own = pltpu.make_async_copy(sbuf.at[me], rbuf.at[me], own_sem.at[0])
-    own.start()
+    def exchange(source, target, g, send_sem, recv_sem):
+        def send(number, carry):
+            step = blocks - number
+            hop = lax.rem(step, 2) * ((step + 1) // 2) + (1 - lax.rem(step, 2)) * (
+                blocks - step // 2
+            )
+            peer = lax.rem(me + hop, blocks)
+            pltpu.make_async_remote_copy(
+                src_ref=source.at[g, peer], dst_ref=target.at[g, me],
+                send_sem=send_sem.at[g], recv_sem=recv_sem.at[g],
+                device_id=(peer, mine), device_id_type=MESH,
+            ).start()
+            return carry
+
+        lax.fori_loop(1, blocks, send, 0)
+
+    def all_of(ref, g, sem):
+        return pltpu.make_async_copy(ref.at[g, rest], ref.at[g, rest], sem.at[g])
+
+    rest = pl.ds(0, blocks - 1)
+    for g in range(2):
+        exchange(sbuf, rbuf, g, send1, recv1)
+    owns = [
+        pltpu.make_async_copy(sbuf.at[g, me], rbuf.at[g, me], own_sem.at[g]) for g in range(2)
+    ]
+    for own in owns:
+        own.start()
 
     loads[2].wait()
     for b in range(width // part):
         columns = slice(b * part, (b + 1) * part)
         gt[columns, :] = turned(gates_ref[:, columns])
-    loads[4].wait()
+    loads[3].wait()
     for j in range(lanes):
         wt[j] = turned(weight_ref[:, j * part : (j + 1) * part]).astype(BF16)
-    for index in (3, 5, 6, 7, 8):
+    for index in (4, 5, 6, 7):
         loads[index].wait()
 
-    own.wait()
-    rest = pl.ds(0, blocks - 1)
-    pltpu.make_async_copy(rbuf.at[rest], rbuf.at[rest], recv1).wait()
-
-    arrived = rbuf[...].astype(F32).reshape(blocks * 2 * narrow, rows)
+    for own in owns:
+        own.wait()
     lane = rows // 2
-    xf[0] = arrived[:, :lane]
-    xf[1] = arrived[:, lane:]
     cos_t, sin_t = twist_ref[0], twist_ref[1]
     cos_2 = jnp.concatenate([cos_t, cos_t], axis=1)
     sin_2 = jnp.concatenate([sin_t, sin_t], axis=1)
-    group = narrow // 2
     lines = group * blocks
 
     def half(g, carry):
+        all_of(rbuf, g, recv1).wait()
+        arrived = rbuf[g].astype(F32).reshape(blocks * narrow, rows)
+        xf[0] = arrived[:, :lane]
+        xf[1] = arrived[:, lane:]
         streams = ([], [])
         for c in range(group):
-            channel = g * group + c
             x = jnp.concatenate(
                 [
-                    xf[side, pl.ds(start + channel, blocks, stride=2 * narrow), :]
-                    for start in (0, narrow)
+                    xf[side, pl.ds(start + c, blocks, stride=narrow), :]
+                    for start in (0, group)
                     for side in range(2)
                 ],
                 axis=1,
@@ -183,7 +204,7 @@
         spectra = mm3(jnp.concatenate(streams[0] + streams[1], axis=0), full_ref)
         vre, vim = spectra[:lines, :rows], spectra[:lines, rows:]
         direct = [
-            jnp.broadcast_to(skip_ref[pl.ds(me * narrow + g * group + c, 1), :], (blocks, rows))
+            jnp.full((blocks, rows), skip_ref[me * narrow + g * group + c], F32)
             for c in range(group)
         ]
         hre = spectra[lines:, :rows] + jnp.concatenate(direct, axis=0)
@@ -202,30 +223,32 @@
         for c in range(group):
             for side in range(2):
                 start = c * rows + side * lane
-                yf[side, pl.ds(g * group + c, blocks, stride=narrow), :] = signal[
+                yf[pl.ds(side * group + c, blocks, stride=narrow), :] = signal[
                     :, start : start + lane
                 ]
+        obuf[g] = yf[...].reshape(blocks, narrow, lane).astype(BF16)
+        exchange(obuf, cbuf, g, send2, recv2)
         return carry
 
     lax.fori_loop(0, 2, half, 0)
-    result = jnp.concatenate([yf[0], yf[1]], axis=1)
-    obuf[...] = result.reshape(blocks, narrow, rows).astype(BF16)
-
-    def send_second(step, carry):
-        peer = lax.rem(me + step, blocks)
-        pltpu.make_async_remote_copy(
-            src_ref=obuf.at[peer], dst_ref=cbuf.at[me], send_sem=send2, recv_sem=recv2,
-            device_id=(peer, mine), device_id_type=MESH,
-        ).start()
-        return carry
-
-    lax.fori_loop(1, blocks, send_second, 0)
-    own = pltpu.make_async_copy(obuf.at[me], cbuf.at[me], own_sem.at[1])
-    own.start()
-    own.wait()
-    pltpu.make_async_copy(cbuf.at[rest], cbuf.at[rest], recv2).wait()
-
-    conv = cbuf[...].astype(F32).reshape(width, rows)
+    owns = [
+        pltpu.make_async_copy(obuf.at[g, me], cbuf.at[g, me], own_sem.at[2 + g]) for g in range(2)
+    ]
+    for own in owns:
+        own.start()
+    for own in owns:
+        own.wait()
+    for g in range(2):
+        all_of(cbuf, g, recv2).wait()
+
+    row_of = lax.broadcasted_iota(jnp.int32, (blocks, narrow, lane), 1)
+    conv = jnp.concatenate(
+        [
+            piece.reshape(width, lane)
+            for piece in paired(cbuf[0].astype(F32), cbuf[1].astype(F32))
+        ],
+        axis=1,
+    )
     gated = (gt[...] * conv).astype(BF16)
 
     def send_third(step, carry):
@@ -248,10 +271,11 @@
     for step in range(1, lanes):
         total = add(step, total)
     fin[...] = total.astype(BF16)
-    done = pltpu.make_async_copy(fin, out_hbm, own_sem.at[2])
+    done = pltpu.make_async_copy(fin, out_hbm, own_sem.at[4])
     done.start()
-    pltpu.make_async_copy(sbuf.at[rest], sbuf.at[rest], send1).wait()
-    pltpu.make_async_copy(obuf.at[rest], obuf.at[rest], send2).wait()
+    for g in range(2):
+        all_of(sbuf, g, send1).wait()
+        all_of(obuf, g, send2).wait()
     pltpu.make_async_copy(pbuf.at[others], pbuf.at[others], send3).wait()
     done.wait()
 
@@ -264,34 +288,33 @@
     anywhere = pl.BlockSpec(memory_space=pl.ANY)
     vmem = pltpu.VMEM
     dma = pltpu.SemaphoreType.DMA
-    operands = (values, gates, taps, skip[:, None], weight, outer, full, final, twist)
+    operands = (values, gates, taps, skip, weight, outer, full, final, twist)
     return pl.pallas_call(
         functools.partial(kernel, blocks, lanes),
         out_shape=jax.ShapeDtypeStruct((features // lanes, rows), BF16),
-        in_specs=[anywhere] * len(operands),
+        in_specs=[anywhere] * 3 + [pl.BlockSpec(memory_space=pltpu.SMEM)] + [anywhere] * 5,
         out_specs=anywhere,
         scratch_shapes=[
             vmem(values.shape, BF16),
             vmem(gates.shape, BF16),
             vmem(taps.shape, BF16),
-            vmem((width, 1), F32),
             vmem(weight.shape, BF16),
             vmem(outer.shape, BF16),
             vmem(full.shape, BF16),
             vmem(final.shape, BF16),
             vmem(twist.shape, F32),
-            vmem((blocks, 2 * narrow, rows), BF16),
-            vmem((blocks, 2 * narrow, rows), BF16),
-            vmem((2, blocks * 2 * narrow, rows // 2), F32),
+            vmem((2, blocks, narrow, rows), BF16),
+            vmem((2, blocks, narrow, rows), BF16),
             vmem((2, blocks * narrow, rows // 2), F32),
-            vmem((blocks, narrow, rows), BF16),
-            vmem((blocks, narrow, rows), BF16),
+            vmem((blocks * narrow, rows // 2), F32),
+            vmem((2, blocks, narrow, rows // 2), BF16),
+            vmem((2, blocks, narrow, rows // 2), BF16),
             vmem((width, rows), F32),
             vmem((lanes, features // lanes, depth), BF16),
             vmem((lanes, features // lanes, rows), BF16),
             vmem((lanes, features // lanes, rows), BF16),
             vmem((features // lanes, rows), BF16),
-            dma((9,)), dma, dma, dma, dma, dma, dma, dma((3,)),
+            dma((8,)), dma((2,)), dma((2,)), dma((2,)), dma((2,)), dma, dma, dma((5,)),
         ],
         compiler_params=pltpu.CompilerParams(
             collective_id=0, has_side_effects=True, vmem_limit_bytes=56 * 2**20

time: 80.7 us -> 71.3 us (0.88)
  Pallas kernels: 77.5 us -> 69.6 us
  local copies, waits for them, and re-layouts: 3.09 us -> 1.57 us
    pallas_call x1, Pallas kernels: 77.5 us -> 69.6 us  [local(): pl.pallas_call(functools.partial(kernel, blocks, lanes), out_shape=jax.Sh...]
    broadcast_in_dim x1 -> x0, local copies, waits for them, and re-layouts: 1.52 us -> none  [local(): skip[:, None]]
where the time goes in v2:
time: 71.3 us; the launch traced here: 71.2 us
  Pallas kernels  69.6 us (98%)
  local copies, waits for them, and re-layouts  1.57 us (2%)
    pallas_call x1, Pallas kernels, local(): pl.pallas_call(functools.partial(kernel, blocks, lanes), out_shape=jax.Sh...  69.6 us
    unnamed x1, local copies, waits for them, and re-layouts  1.57 us

profile of v2, /device:TPU:1, one launch (start us, length us, event | category | flops | bytes accessed | tf_op | source)
XLA Modules:
  0.0 71.2 jit_solution(18099521578072421870)
XLA Ops:
  0.0 69.6 %hyena.1 = bf16[256,256]{1,0:T(8,128)(2,1)} custom-call(bf16[256,512]{1,0:T(8,128)(2,1)} %values_hbm.1, bf16[256,512]{1,0:T(8,128)(2,1)} %gates_hbm.1, bf16[256,512]{1,0:T(8,128)(2,1)} %taps_hbm.1, f32[512]{0:T(512)} %skip_ref.1, bf16[512,2048]{1,0:T(8,128)(2,1)} %weight_hbm.1, bf16[2,128,64]{2,1,0:T(8,128)(2,1)} %constant.8.clone.outer_hbm, ...), custom_call_target="tpu_custom_call" | custom-call | tf_op jit(solution)/shard_map/hyena/pallas_call | solution.py:292
  69.6 1.6 %copy.11 = bf16[256,256]{1,0:T(8,128)(2,1)} copy(bf16[256,256]{1,0:T(8,128)(2,1)} %hyena.1) | data formatting | bytes 262144

commit v3 on v2

--- a/solution.py
+++ b/solution.py
@@ -57,15 +57,16 @@
     blocks, lanes,
     values_hbm, gates_hbm, taps_hbm, skip_ref, weight_hbm,
     outer_hbm, full_hbm, final_hbm, twist_hbm,
-    out_hbm,
+    out_ref,
     values_ref, gates_ref, taps_ref, weight_ref,
     outer_ref, full_ref, final_ref, twist_ref,
-    sbuf, rbuf, xf, yf, obuf, cbuf, gt, wt, pbuf, qbuf, fin,
-    load_sem, send1, recv1, send2, recv2, send3, recv3, own_sem,
+    sbuf, rbuf, xf, yf, obuf, cbuf, gt, wall, wsib, gated, gsib, acc, ubuf, tbuf,
+    load_sem, send1, recv1, send2, recv2, pair_send, pair_recv, send4, recv4, own_sem,
 ):
     me = lax.axis_index("seq")
     mine = lax.axis_index("chan")
     rows, width = values_ref.shape
+    rows_out = out_ref.shape[0]
     narrow = width // blocks
 
     loads = []
@@ -123,51 +124,61 @@
             jnp.where(low, pltpu.roll(first, group, 1), second),
         )
 
-    for b in range(width // part):
-        columns = slice(b * part, (b + 1) * part)
-        v = turned(values_ref[:, columns])
-        h = turned(taps_ref[:, columns])
-        both = paired(v.reshape(per, narrow, rows), h.reshape(per, narrow, rows))
-        for g in range(2):
-            sbuf[g, b * per : (b + 1) * per] = both[g].astype(BF16)
+    for g in range(2):
+        columns = slice(g * part, (g + 1) * part)
+        v = turned(values_ref[:, columns]).reshape(per, narrow, rows)
+        h = turned(taps_ref[:, columns]).reshape(per, narrow, rows)
+        both = jnp.stack(paired(v, h), axis=1).reshape(blocks, narrow, rows)
+        sbuf[g] = both.astype(BF16)
 
     pl.semaphore_wait(barrier, blocks + lanes - 2)
 
-    def exchange(source, target, g, send_sem, recv_sem):
-        def send(number, carry):
-            step = blocks - number
-            hop = lax.rem(step, 2) * ((step + 1) // 2) + (1 - lax.rem(step, 2)) * (
-                blocks - step // 2
-            )
-            peer = lax.rem(me + hop, blocks)
+    def exchange(source, target, send_sem, recv_sem):
+        def send(hop):
+            peer = me + hop
+            peer = jnp.where(peer >= blocks, peer - blocks, peer)
             pltpu.make_async_remote_copy(
-                src_ref=source.at[g, peer], dst_ref=target.at[g, me],
-                send_sem=send_sem.at[g], recv_sem=recv_sem.at[g],
+                src_ref=source.at[peer], dst_ref=target.at[me],
+                send_sem=send_sem, recv_sem=recv_sem,
                 device_id=(peer, mine), device_id_type=MESH,
             ).start()
+
+        def pair(step, carry):
+            send(blocks // 2 - step)
+            send(blocks // 2 + step)
             return carry
 
-        lax.fori_loop(1, blocks, send, 0)
-
-    def all_of(ref, g, sem):
-        return pltpu.make_async_copy(ref.at[g, rest], ref.at[g, rest], sem.at[g])
+        send(blocks // 2)
+        lax.fori_loop(1, blocks // 2, pair, 0)
+
+    def all_of(ref, sem):
+        return pltpu.make_async_copy(ref.at[rest], ref.at[rest], sem)
 
     rest = pl.ds(0, blocks - 1)
     for g in range(2):
-        exchange(sbuf, rbuf, g, send1, recv1)
+        exchange(sbuf.at[g], rbuf.at[g], send1.at[g], recv1.at[g])
     owns = [
         pltpu.make_async_copy(sbuf.at[g, me], rbuf.at[g, me], own_sem.at[g]) for g in range(2)
     ]
     for own in owns:
         own.start()
 
+    chips = lanes // 2
+    chip = mine // 2
+    core = lax.rem(mine, 2)
+    sibling = (me, 2 * chip + 1 - core)
+
     loads[2].wait()
-    for b in range(width // part):
-        columns = slice(b * part, (b + 1) * part)
-        gt[columns, :] = turned(gates_ref[:, columns])
+    for g in range(2):
+        columns = slice(g * part, (g + 1) * part)
+        gt[g] = turned(gates_ref[:, columns])
     loads[3].wait()
     for j in range(lanes):
-        wt[j] = turned(weight_ref[:, j * part : (j + 1) * part]).astype(BF16)
+        wall[j % 2, j // 2] = turned(weight_ref[:, j * part : (j + 1) * part]).astype(BF16)
+    pltpu.make_async_remote_copy(
+        src_ref=wall.at[1 - core], dst_ref=wsib, send_sem=pair_send.at[2],
+        recv_sem=pair_recv.at[2], device_id=sibling, device_id_type=MESH,
+    ).start()
     for index in (4, 5, 6, 7):
         loads[index].wait()
 
@@ -180,7 +191,7 @@
     lines = group * blocks
 
     def half(g, carry):
-        all_of(rbuf, g, recv1).wait()
+        all_of(rbuf.at[g], recv1.at[g]).wait()
         arrived = rbuf[g].astype(F32).reshape(blocks * narrow, rows)
         xf[0] = arrived[:, :lane]
         xf[1] = arrived[:, lane:]
@@ -204,7 +215,7 @@
         spectra = mm3(jnp.concatenate(streams[0] + streams[1], axis=0), full_ref)
         vre, vim = spectra[:lines, :rows], spectra[:lines, rows:]
         direct = [
-            jnp.full((blocks, rows), skip_ref[me * narrow + g * group + c], F32)
+            jnp.full((blocks, rows), skip_ref[g * part + me * group + c], F32)
             for c in range(group)
         ]
         hre = spectra[lines:, :rows] + jnp.concatenate(direct, axis=0)
@@ -227,7 +238,7 @@
                     :, start : start + lane
                 ]
         obuf[g] = yf[...].reshape(blocks, narrow, lane).astype(BF16)
-        exchange(obuf, cbuf, g, send2, recv2)
+        exchange(obuf.at[g], cbuf.at[g], send2.at[g], recv2.at[g])
         return carry
 
     lax.fori_loop(0, 2, half, 0)
@@ -238,46 +249,79 @@
         own.start()
     for own in owns:
         own.wait()
-    for g in range(2):
-        all_of(cbuf, g, recv2).wait()
-
-    row_of = lax.broadcasted_iota(jnp.int32, (blocks, narrow, lane), 1)
-    conv = jnp.concatenate(
-        [
-            piece.reshape(width, lane)
-            for piece in paired(cbuf[0].astype(F32), cbuf[1].astype(F32))
-        ],
-        axis=1,
-    )
-    gated = (gt[...] * conv).astype(BF16)
-
-    def send_third(step, carry):
-        peer = lax.rem(mine + step, lanes)
-        pbuf[peer] = mm(wt[peer], gated).astype(BF16)
+
+    pair_copies = []
+    order = [2, 1, 3, 0]
+    row_of = lax.broadcasted_iota(jnp.int32, (per, narrow, lane), 1)
+    for g in range(2):
+        all_of(cbuf.at[g], recv2.at[g]).wait()
+        back = cbuf[g].astype(F32).reshape(per, 2, narrow, lane)
+        pieces = paired(back[:, 0], back[:, 1])
+        conv = jnp.concatenate([piece.reshape(part, lane) for piece in pieces], axis=1)
+        gated[g] = (gt[g] * conv).astype(BF16)
+        copy = pltpu.make_async_remote_copy(
+            src_ref=gated.at[g], dst_ref=gsib.at[g], send_sem=pair_send.at[g],
+            recv_sem=pair_recv.at[g], device_id=sibling, device_id_type=MESH,
+        )
+        copy.start()
+        pair_copies.append(copy)
+        columns = slice(g * part, (g + 1) * part)
+        for hop in order:
+            there = lax.rem(chip + hop, chips)
+            term = mm(wall[core, there, :, columns], gated[g])
+            acc[hop] = term if g == 0 else acc[hop] + term
+        if g == 0:
+            pltpu.make_async_copy(wsib, wsib, pair_recv.at[2]).wait()
+            copy.wait_recv()
+            for hop in order:
+                there = lax.rem(chip + hop, chips)
+                acc[hop] = acc[hop] + mm(wsib[there, :, columns], gsib[g])
+    columns = slice(part, 2 * part)
+    pair_copies[1].wait_recv()
+    middle = rows_out // 2
+    own_half = [slice(0, middle), slice(middle, rows_out)]
+
+    def pass_on(way, stage, value, target):
+        ubuf[way, stage] = value.astype(BF16)
+        there = lax.rem(chip + (1, chips - 1)[way], chips)
         pltpu.make_async_remote_copy(
-            src_ref=pbuf.at[peer], dst_ref=qbuf.at[mine], send_sem=send3, recv_sem=recv3,
-            device_id=(me, peer), device_id_type=MESH,
+            src_ref=ubuf.at[way, stage], dst_ref=target, send_sem=send4,
+            recv_sem=recv4.at[way, stage], device_id=(me, 2 * there + core),
+            device_id_type=MESH,
         ).start()
-        return carry
-
-    lax.fori_loop(1, lanes, send_third, 0)
-    total = mm(wt[mine], gated)
-    others = pl.ds(0, lanes - 1)
-    pltpu.make_async_copy(qbuf.at[others], qbuf.at[others], recv3).wait()
-
-    def add(step, running):
-        return running + qbuf[lax.rem(mine + step, lanes)].astype(F32)
-
-    for step in range(1, lanes):
-        total = add(step, total)
-    fin[...] = total.astype(BF16)
-    done = pltpu.make_async_copy(fin, out_hbm, own_sem.at[4])
-    done.start()
-    for g in range(2):
-        all_of(sbuf, g, send1).wait()
-        all_of(obuf, g, send2).wait()
-    pltpu.make_async_copy(pbuf.at[others], pbuf.at[others], send3).wait()
-    done.wait()
+
+    def came(way, stage, ref):
+        pltpu.make_async_copy(ref, ref, recv4.at[way, stage]).wait()
+
+    def finished(hop):
+        there = lax.rem(chip + hop, chips)
+        return acc[hop] + mm(wsib[there, :, columns], gsib[1])
+
+    far = finished(2)
+    for way in range(2):
+        pass_on(way, 0, far[own_half[way]], tbuf.at[way, 0])
+    near = []
+    for way, hop in ((0, 1), (1, 3)):
+        near.append(finished(hop))
+        pass_on(way, 1, near[way][own_half[1 - way]], tbuf.at[way, 1])
+    total = finished(0)
+    for way in range(2):
+        came(way, 0, tbuf.at[way, 0])
+        merged = near[way][own_half[way]] + tbuf[way, 0].astype(F32)
+        pass_on(way, 2, merged, tbuf.at[way, 2])
+    for way in range(2):
+        came(way, 1, tbuf.at[way, 1])
+    for way in range(2):
+        came(way, 2, tbuf.at[way, 2])
+        out_ref[own_half[way], :] = (
+            total[own_half[way]] + tbuf[way, 2].astype(F32) + tbuf[1 - way, 1].astype(F32)
+        ).astype(out_ref.dtype)
+    for g in range(2):
+        all_of(sbuf.at[g], send1.at[g]).wait()
+        all_of(obuf.at[g], send2.at[g]).wait()
+        pair_copies[g].wait_send()
+    pltpu.make_async_copy(wsib, wsib, pair_send.at[2]).wait()
+    pltpu.make_async_copy(ubuf, ubuf, send4).wait()
 
 
 def local(blocks, lanes, values, gates, taps, skip, weight):
@@ -293,7 +337,7 @@
         functools.partial(kernel, blocks, lanes),
         out_shape=jax.ShapeDtypeStruct((features // lanes, rows), BF16),
         in_specs=[anywhere] * 3 + [pl.BlockSpec(memory_space=pltpu.SMEM)] + [anywhere] * 5,
-        out_specs=anywhere,
+        out_specs=pl.BlockSpec(memory_space=pltpu.VMEM),
         scratch_shapes=[
             vmem(values.shape, BF16),
             vmem(gates.shape, BF16),
@@ -309,12 +353,16 @@
             vmem((blocks * narrow, rows // 2), F32),
             vmem((2, blocks, narrow, rows // 2), BF16),
             vmem((2, blocks, narrow, rows // 2), BF16),
-            vmem((width, rows), F32),
-            vmem((lanes, features // lanes, depth), BF16),
-            vmem((lanes, features // lanes, rows), BF16),
-            vmem((lanes, features // lanes, rows), BF16),
-            vmem((features // lanes, rows), BF16),
-            dma((8,)), dma((2,)), dma((2,)), dma((2,)), dma((2,)), dma, dma, dma((5,)),
+            vmem((2, width // 2, rows), F32),
+            vmem((2, lanes // 2, features // lanes, depth), BF16),
+            vmem((lanes // 2, features // lanes, depth), BF16),
+            vmem((2, width // 2, rows), BF16),
+            vmem((2, width // 2, rows), BF16),
+            vmem((lanes // 2, features // lanes, rows), F32),
+            vmem((2, 3, features // lanes // 2, rows), BF16),
+            vmem((2, 3, features // lanes // 2, rows), BF16),
+            dma((8,)), dma((2,)), dma((2,)), dma((2,)), dma((2,)),
+            dma((3,)), dma((3,)), dma, dma((2, 3)), dma((4,)),
         ],
         compiler_params=pltpu.CompilerParams(
             collective_id=0, has_side_effects=True, vmem_limit_bytes=56 * 2**20

time: 71.3 us -> 69 us (0.968)
  Pallas kernels: 69.6 us -> 67.2 us
    pallas_call x1, Pallas kernels: 69.6 us -> 67.2 us  [local(): pl.pallas_call(functools.partial(kernel, blocks, lanes), out_shape=jax.Sh...]
where the time goes in v3:
time: 69 us; the launch traced here: 68.8 us
  Pallas kernels  67.2 us (97%)
  local copies, waits for them, and re-layouts  1.57 us (2%)
    pallas_call x1, Pallas kernels, local(): pl.pallas_call(functools.partial(kernel, blocks, lanes), out_shape=jax.Sh...  67.2 us
    unnamed x1, local copies, waits for them, and re-layouts  1.57 us

profile of v3, /device:TPU:1, one launch (start us, length us, event | category | flops | bytes accessed | tf_op | source)
XLA Modules:
  0.0 68.8 jit_solution(14835618782099747224)
XLA Ops:
  0.0 67.2 %hyena.1 = bf16[256,256]{1,0:T(8,128)(2,1)} custom-call(bf16[256,512]{1,0:T(8,128)(2,1)} %values_hbm.1, bf16[256,512]{1,0:T(8,128)(2,1)} %gates_hbm.1, bf16[256,512]{1,0:T(8,128)(2,1)} %taps_hbm.1, f32[512]{0:T(512)} %skip_ref.1, bf16[512,2048]{1,0:T(8,128)(2,1)} %weight_hbm.1, bf16[2,128,64]{2,1,0:T(8,128)(2,1)} %constant.8.clone.outer_hbm, ...), custom_call_target="tpu_custom_call" | custom-call | tf_op jit(solution)/shard_map/hyena/pallas_call | solution.py:336
  67.2 1.6 %copy.11 = bf16[256,256]{1,0:T(8,128)(2,1)} copy(bf16[256,256]{1,0:T(8,128)(2,1)} %hyena.1) | data formatting | bytes 262144

commit v4 on v3

--- a/solution.py
+++ b/solution.py
@@ -55,10 +55,10 @@
 
 def kernel(
     blocks, lanes,
-    values_hbm, gates_hbm, taps_hbm, skip_ref, weight_hbm,
+    values_hbm, gates_hbm, taps_hbm, skip_hbm, weight_hbm,
     outer_hbm, full_hbm, final_hbm, twist_hbm,
     out_ref,
-    values_ref, gates_ref, taps_ref, weight_ref,
+    values_ref, gates_ref, taps_ref, skip_ref, weight_ref,
     outer_ref, full_ref, final_ref, twist_ref,
     sbuf, rbuf, xf, yf, obuf, cbuf, gt, wall, wsib, gated, gsib, acc, ubuf, tbuf,
     load_sem, send1, recv1, send2, recv2, pair_send, pair_recv, send4, recv4, own_sem,
@@ -80,6 +80,7 @@
             (full_hbm, full_ref),
             (final_hbm, final_ref),
             (twist_hbm, twist_ref),
+            (skip_hbm, skip_ref),
         )
     ):
         copy = pltpu.make_async_copy(source, target, load_sem.at[index])
@@ -88,10 +89,14 @@
 
     barrier = pltpu.get_barrier_semaphore()
 
+    def greet(hop):
+        peer = me + hop
+        peer = jnp.where(peer >= blocks, peer - blocks, peer)
+        pl.semaphore_signal(barrier, inc=1, device_id=(peer, mine), device_id_type=MESH)
+
     def greet_seq(step, carry):
-        pl.semaphore_signal(
-            barrier, inc=1, device_id=(lax.rem(me + step, blocks), mine), device_id_type=MESH
-        )
+        greet(blocks // 2 - step)
+        greet(blocks // 2 + step)
         return carry
 
     def greet_chan(step, carry):
@@ -100,7 +105,8 @@
         )
         return carry
 
-    lax.fori_loop(1, blocks, greet_seq, 0)
+    greet(blocks // 2)
+    lax.fori_loop(1, blocks // 2, greet_seq, 0)
     lax.fori_loop(1, lanes, greet_chan, 0)
 
     part = 256
@@ -179,7 +185,7 @@
         src_ref=wall.at[1 - core], dst_ref=wsib, send_sem=pair_send.at[2],
         recv_sem=pair_recv.at[2], device_id=sibling, device_id_type=MESH,
     ).start()
-    for index in (4, 5, 6, 7):
+    for index in (4, 5, 6, 7, 8):
         loads[index].wait()
 
     for own in owns:
@@ -336,12 +342,13 @@
     return pl.pallas_call(
         functools.partial(kernel, blocks, lanes),
         out_shape=jax.ShapeDtypeStruct((features // lanes, rows), BF16),
-        in_specs=[anywhere] * 3 + [pl.BlockSpec(memory_space=pltpu.SMEM)] + [anywhere] * 5,
+        in_specs=[anywhere] * len(operands),
         out_specs=pl.BlockSpec(memory_space=pltpu.VMEM),
         scratch_shapes=[
             vmem(values.shape, BF16),
             vmem(gates.shape, BF16),
             vmem(taps.shape, BF16),
+            pltpu.SMEM(skip.shape, F32),
             vmem(weight.shape, BF16),
             vmem(outer.shape, BF16),
             vmem(full.shape, BF16),
@@ -361,7 +368,7 @@
             vmem((lanes // 2, features // lanes, rows), F32),
             vmem((2, 3, features // lanes // 2, rows), BF16),
             vmem((2, 3, features // lanes // 2, rows), BF16),
-            dma((8,)), dma((2,)), dma((2,)), dma((2,)), dma((2,)),
+            dma((9,)), dma((2,)), dma((2,)), dma((2,)), dma((2,)),
             dma((3,)), dma((3,)), dma, dma((2, 3)), dma((4,)),
         ],
         compiler_params=pltpu.CompilerParams(

time: 69 us -> 67.7 us (0.981)
  Pallas kernels: 67.2 us -> 66 us
    pallas_call x1, Pallas kernels: 67.2 us -> 66 us  [local(): pl.pallas_call(functools.partial(kernel, blocks, lanes), out_shape=jax.Sh...]
where the time goes in v4:
time: 67.7 us; the launch traced here: 67.6 us
  Pallas kernels  66 us (97%)
  local copies, waits for them, and re-layouts  1.57 us (2%)
    pallas_call x1, Pallas kernels, local(): pl.pallas_call(functools.partial(kernel, blocks, lanes), out_shape=jax.Sh...  66 us
    unnamed x1, local copies, waits for them, and re-layouts  1.57 us

profile of v4, /device:TPU:1, one launch (start us, length us, event | category | flops | bytes accessed | tf_op | source)
XLA Modules:
  0.0 67.6 jit_solution(18078296545082692659)
XLA Ops:
  0.0 66.0 %hyena.1 = bf16[256,256]{1,0:T(8,128)(2,1)} custom-call(bf16[256,512]{1,0:T(8,128)(2,1)} %values_hbm.1, bf16[256,512]{1,0:T(8,128)(2,1)} %gates_hbm.1, bf16[256,512]{1,0:T(8,128)(2,1)} %taps_hbm.1, f32[512]{0:T(512)} %skip_hbm.1, bf16[512,2048]{1,0:T(8,128)(2,1)} %weight_hbm.1, bf16[2,128,64]{2,1,0:T(8,128)(2,1)} %constant.8.clone.outer_hbm, ...), custom_call_target="tpu_custom_call" | custom-call | tf_op jit(solution)/shard_map/hyena/pallas_call | solution.py:342
  66.0 1.6 %copy.11 = bf16[256,256]{1,0:T(8,128)(2,1)} copy(bf16[256,256]{1,0:T(8,128)(2,1)} %hyena.1) | data formatting | bytes 262144
